TPU v7x, 256 devices: a whole 4x4x8 slice. The times are simulated.
256 devices in a mesh: gz: 8 (over x, core), ty: 8 (over z), tx: 4 (over y).
Axes of the slice: x: 4, y: 4, z: 8, core: 2. Of those that a mesh axis runs over, the one named last changes fastest.
Arguments:
- images: bfloat16 [8, 4096, 2048], P('gz', 'ty', 'tx'), may hold values from -40 to 40, as said below
- boundary: bfloat16 [4096, 2048], P('ty', 'tx'), may hold values from -40 to 40, as said below
- anchor: float32 [8, 1024, 512], P('gz', 'ty', 'tx'), may hold values from 0.02 to 0.5
Outputs:
- mesh_shift: float32 [8, 2, 1024, 512], P('gz', None, 'ty', 'tx')
- drift: float32 [8, 8, 4, 2, 128], P('gz', 'ty', 'tx')
Inputs may be any that keep to these rules, and one draw needn't show every extreme that they name: `images`: pixel intensities. `boundary`: pixel intensities.
All inputs are finite; a program needn't handle non-finite values.
Results may differ from a plain program's by a relative error of at most 0.0003.
Values may be sent and summed in bfloat16 or wider, within the bound.
A program may use at most 64 MiB of HBM per device.

v0:
```python
import functools
import math

import jax
import jax.numpy as jnp
import numpy as np
from jax import lax
from jax.experimental import pallas as pl
from jax.experimental.pallas import tpu as pltpu
from jax.sharding import PartitionSpec as P

PATCH = 128
STRIDE = 4
SWEEPS = 32
TILE = 512
NODES = 128
PER = TILE // PATCH
WIDE = NODES + 2 * SWEEPS
GROUPS = WIDE // 8
LANES = 2 * WIDE

f32 = jnp.float32
bf16 = jnp.bfloat16
MESH = pl.DeviceIdType.MESH
AROUND = [(dy, dx) for dy in (-1, 0, 1) for dx in (-1, 0, 1)]


def slot(dy, dx):
    return (dy + 1) * 3 + dx + 1


def pieces(table, count):
    parts = []
    rest = np.asarray(table, np.float64)
    for _ in range(count):
        part = rest.astype(jnp.bfloat16)
        parts.append(part)
        rest = rest - part.astype(np.float64)
    return parts


def spread_table():
    pos = (np.arange(NODES) + 0.5) * STRIDE / PATCH - 0.5
    weights = np.maximum(0.0, 1.0 - np.abs(pos[:, None] - np.arange(PER)[None, :]))
    return weights / weights.sum(axis=1, keepdims=True)


def tables():
    half = PATCH // 2
    n = np.arange(PATCH)
    angle = lambda k: 2.0 * np.pi * (n[:, None] * k[None, :] % PATCH) / PATCH
    low, high = np.arange(half), np.arange(1, half)
    cos_low, sin_high = np.cos(angle(low)), np.sin(angle(high))
    last = np.cos(np.pi * n)[:, None]
    zero = np.zeros_like(last)
    basis = np.concatenate([cos_low, last, sin_high], axis=1)
    same = np.concatenate([cos_low, last, cos_low[:, 1:]], axis=1)
    cross = np.concatenate([zero, sin_high, zero, -sin_high], axis=1)
    weight = np.full(PATCH, 2.0 / PATCH)
    weight[[0, half]] = 1.0 / PATCH
    inverse = basis * weight[None, :]

    b_hi, b_lo = pieces(basis, 2)
    s_hi, s_lo = pieces(same, 2)
    c_hi, c_lo = pieces(cross, 2)
    r_hi, r_lo = pieces(inverse.T, 2)
    l_hi, l_lo = pieces(inverse * (math.log2(math.e) / PATCH), 2)
    left = np.concatenate([b_hi.T, b_lo.T], axis=0)
    right = np.concatenate([b_hi, b_lo], axis=1)
    right_pair = np.concatenate([s_hi, c_hi, s_lo, c_lo], axis=1)
    back_right = np.concatenate([r_hi, r_lo], axis=1)
    back_left = np.concatenate([l_hi, l_lo], axis=0)
    twice = lambda t, axis: np.concatenate([t, t], axis=axis)

    spread = spread_table()
    spread_lanes = np.repeat(spread.T, PER, axis=0).astype(np.float32)
    rows = np.zeros((WIDE, 128))
    for group in range(GROUPS):
        for sub in range(8):
            i = sub * GROUPS + group - SWEEPS
            dy = i // NODES
            for piece in range(3):
                first = piece * 32 + (dy + 1) * 8
                rows[group * 8 + sub, first : first + PER] = spread[i - dy * NODES]
    return (
        left,
        twice(right, 0),
        twice(right_pair, 0),
        twice(back_right, 0),
        twice(back_left, 1),
        spread_lanes,
        rows.astype(jnp.bfloat16),
    )


def mm(a, b):
    return jnp.dot(a, b, preferred_element_type=f32)


def halves(value):
    hi = value.astype(bf16)
    return hi, (value - hi.astype(f32)).astype(bf16)


def iota(shape, dim):
    return lax.broadcasted_iota(jnp.int32, shape, dim)


def stacked_rows(wide):
    return jnp.concatenate([wide[:, q * PATCH : (q + 1) * PATCH] for q in range(PER)], axis=0)


def side_by_side(tall):
    return jnp.concatenate([tall[q * PATCH : (q + 1) * PATCH] for q in range(PER)], axis=1)


def row_pass(pixels, left):
    both = mm(left[...], pixels)
    return jnp.concatenate(halves(stacked_rows(both[:PATCH] + both[PATCH:])), axis=1)


def packed_spectrum(pixels, left, right):
    both = mm(row_pass(pixels, left), right[...])
    return both[:, :PATCH] + both[:, PATCH:]


def paired_spectrum(pixels, left, right_pair):
    both = mm(row_pass(pixels, left), right_pair[...])
    return (
        both[:, :PATCH] + both[:, 2 * PATCH : 3 * PATCH],
        both[:, PATCH : 2 * PATCH] + both[:, 3 * PATCH :],
    )


def cross_spectrum(pair, later):
    half = PATCH // 2
    same, cross = pair
    turned = pltpu.roll(later, half, 1)
    first = iota((half, PATCH), 0) == 0
    out = []
    for q in range(PER):
        top = slice(q * PATCH, q * PATCH + half)
        low = slice(q * PATCH + half, (q + 1) * PATCH)
        joint = lambda e, c: same[e] * later[c] + cross[e] * turned[c]
        low_low = joint(low, low)
        out.append(joint(top, top) + jnp.where(first, 0.0, low_low))
        out.append(jnp.where(first, low_low, joint(top, low) - joint(low, top)))
    return jnp.concatenate(out, axis=0)


def scores(product, back_right, back_left):
    both = mm(jnp.concatenate(halves(product), axis=1), back_right[...])
    wide = side_by_side(both[:, :PATCH] + both[:, PATCH:])
    both = mm(back_left[...], jnp.concatenate(halves(wide), axis=0))
    return both[:PATCH] + both[PATCH:]


def signed_lag(shape, dim):
    lag = iota(shape, dim)
    return jnp.where(lag < PATCH // 2, lag, lag - PATCH).astype(f32)


def hat(offset):
    return jnp.maximum(0.0, 1.0 - jnp.abs(offset))


def widen(left, here, right, lane):
    turn = lambda v: pltpu.roll(v, 64, 1)
    centre = turn(here[1])
    return (
        here[0],
        jnp.where(lane < 32, right[0], jnp.where(lane < 64, turn(left[1]), centre)),
        jnp.where(lane < 64, centre, jnp.where(lane < 96, turn(right[1]), left[0])),
    )


def kernel(
    sizes,
    images, boundary, anchor, left, right, right_pair, back_right, back_left, spread_lanes, spread_rows,
    mesh_out, drift_out,
    own, before, after, anchors, patch_in, patch_out, sums, land_in, land_out,
    rate_rows, pull_rows, rate, pull, mesh_a, mesh_b, natural,
    own_sem, before_sem, after_sem, up_sem, down_sem, anchor_sem, anchor_sent, anchor_own,
    patch_sem, patch_sent, land_sem, land_sent,
):
    n_gz, n_ty, n_tx = sizes
    g, y, x = lax.axis_index("gz"), lax.axis_index("ty"), lax.axis_index("tx")

    def inside(dy, dx):
        ok = None
        for pos, step, count in ((y, dy, n_ty), (x, dx, n_tx)):
            if step:
                here = (pos + step >= 0) & (pos + step < count)
                ok = here if ok is None else ok & here
        return (g >= 0) if ok is None else ok

    def band(ref, r):
        return ref.at[pl.ds(pl.multiple_of(r * PATCH, PATCH), PATCH), :]

    for r in range(PER):
        pltpu.make_async_copy(band(images.at[0], r), own.at[r], own_sem.at[r]).start()

        @pl.when(g == 0)
        def _():
            pltpu.make_async_copy(band(boundary, r), before.at[r], before_sem.at[r]).start()

        @pl.when(g == n_gz - 1)
        def _():
            pltpu.make_async_copy(band(boundary, r), after.at[r], after_sem.at[r]).start()

    pltpu.make_async_copy(anchor.at[0], anchors.at[slot(0, 0)], anchor_own).start()

    barrier = pltpu.get_barrier_semaphore()
    greeted = jnp.int32(0)

    def greet(ok, device):
        @pl.when(ok)
        def _():
            pl.semaphore_signal(barrier, inc=1, device_id=device, device_id_type=MESH)

        return jnp.where(ok, 1, 0).astype(jnp.int32)

    for dz in (-1, 1, 0):
        for dy, dx in AROUND:
            if (dz, dy, dx) != (0, 0, 0):
                ok = inside(dy, dx) & (g + dz >= 0) & (g + dz < n_gz)
                greeted += greet(ok, (g + dz, y + dy, x + dx))
    for step in range(2, n_gz):
        greeted += greet(g + step < n_gz, (g + step, y, x))
        greeted += greet(g - step >= 0, (g - step, y, x))

    ramp_rows = iota((16, NODES), 1).astype(f32)
    for t in range(n_gz):

        @pl.when(t >= g)
        def _():
            land_in[t] = ramp_rows

    for dy, dx in AROUND:
        if (dy, dx) != (0, 0):

            @pl.when(jnp.logical_not(inside(dy, dx)))
            def _():
                anchors[slot(dy, dx)] = jnp.zeros((NODES, NODES), f32)
                patch_in[slot(dy, dx)] = jnp.zeros((8, NODES), f32)

        @pl.when(jnp.logical_not(inside(dy, dx)) | (g < 2))
        def _():
            patch_in[9 + slot(dy, dx)] = jnp.zeros((8, NODES), f32)

    pl.semaphore_wait(barrier, greeted)

    def remote(src, dst, sent, arrived, device):
        return pltpu.make_async_remote_copy(
            src_ref=src, dst_ref=dst, send_sem=sent, recv_sem=arrived, device_id=device, device_id_type=MESH
        )

    def to_later(r):
        return remote(band(images.at[0], r), before.at[r], up_sem.at[r], before_sem.at[r], (g + 1, y, x))

    def to_earlier(r):
        return remote(band(images.at[0], r), after.at[r], down_sem.at[r], after_sem.at[r], (g - 1, y, x))

    for r in range(PER):

        @pl.when(g < n_gz - 1)
        def _():
            to_later(r).start()

        @pl.when(g > 0)
        def _():
            to_earlier(r).start()

    rows_of = {-1: (0, SWEEPS), 0: (0, NODES), 1: (NODES - SWEEPS, SWEEPS)}

    def anchor_copy(dy, dx):
        first, count = rows_of[dy]
        to = slot(-dy, -dx)
        return remote(
            anchor.at[0, pl.ds(first, count), :],
            anchors.at[to, pl.ds(first, count), :],
            anchor_sent.at[to],
            anchor_sem.at[to],
            (g, y + dy, x + dx),
        )

    for dy, dx in AROUND:
        if (dy, dx) != (0, 0):

            @pl.when(inside(dy, dx))
            def _():
                anchor_copy(dy, dx).start()

    def arrival(ref, sem):
        pltpu.make_async_copy(ref, ref, sem).wait()

    lag_rows = signed_lag((PATCH, PATCH), 0)

    def softmax_sums(wide, pair, r):
        for q in range(PER):
            score = wide[:, q * PATCH : (q + 1) * PATCH]
            weight = jnp.exp2(score - jnp.max(score))
            at = pl.ds(q * PER + r, 1)
            sums[pair, 0, at, :] = jnp.sum(weight, axis=0, keepdims=True)
            sums[pair, 1, at, :] = jnp.sum(weight * lag_rows, axis=0, keepdims=True)

    def band_step(r, carry):
        arrival(own.at[r], own_sem.at[r])
        here = packed_spectrum(own[r], left, right)
        arrival(before.at[r], before_sem.at[r])
        pair = paired_spectrum(before[r], left, right_pair)
        softmax_sums(scores(cross_spectrum(pair, here), back_right, back_left), 0, r)
        arrival(after.at[r], after_sem.at[r])
        there = packed_spectrum(after[r], left, right)
        softmax_sums(scores(cross_spectrum(pair, there), back_right, back_left), 1, r)
        return carry

    lax.fori_loop(0, PER, band_step, 0)

    lag_lanes = signed_lag((PER * PER, PATCH), 1)
    sub8 = iota((8, NODES), 0)

    def flow(pair):
        weight = sums[pair, 0]
        scale = (1.0 / STRIDE) / jnp.sum(weight, axis=1, keepdims=True)
        rows = jnp.sum(sums[pair, 1], axis=1, keepdims=True) * scale
        cols = jnp.sum(weight * lag_lanes, axis=1, keepdims=True) * scale
        return rows, cols

    def spread_tile(rows, cols):
        def over_cols(value):
            part = value * spread_lanes[...]
            part = part[:8] + part[8:]
            return part + pltpu.roll(part, 4, 0)

        return jnp.where(sub8 < 4, over_cols(rows), over_cols(cols))

    near, far = flow(0), flow(1)
    near_scale = jnp.where(g >= 2, 0.5, 1.0).astype(f32)
    mine = spread_tile(*(near_scale * v for v in near))
    patch_in[slot(0, 0)] = mine
    patch_out[0] = mine
    patch_out[1] = spread_tile(*(0.5 * (b - a) for a, b in zip(near, far)))

    def patch_copy(kind, dy, dx):
        to = 9 * kind + slot(-dy, -dx)
        return remote(
            patch_out.at[kind], patch_in.at[to], patch_sent.at[to], patch_sem.at[to], (g + kind, y + dy, x + dx)
        )

    ahead = (g >= 1) & (g < n_gz - 1)
    for dy, dx in AROUND:

        @pl.when(inside(dy, dx) & ahead)
        def _():
            patch_copy(1, dy, dx).start()

        if (dy, dx) != (0, 0):

            @pl.when(inside(dy, dx))
            def _():
                patch_copy(0, dy, dx).start()

    arrival(anchors.at[slot(0, 0)], anchor_own)
    for dy, dx in AROUND:
        if (dy, dx) != (0, 0):
            first, count = rows_of[-dy]
            part = anchors.at[slot(dy, dx), pl.ds(first, count), :]

            @pl.when(inside(dy, dx))
            def _():
                arrival(part, anchor_sem.at[slot(dy, dx)])

    top = 0
    for dy in (-1, 0, 1):
        first, count = rows_of[-dy]
        lane = iota((count, NODES), 1)
        rates, pulls = [], []
        for dx in (-1, 0, 1):
            tie = anchors[slot(dy, dx), pl.ds(first, count), :]
            held = 1.0 / (4.0 + tie)
            if (dy, dx) != (0, 0):
                held = held * jnp.where(inside(dy, dx), 1.0, 0.0).astype(f32)
            rates.append((held, held))
            pulls.append((tie * held,) * 2)
        for ref, parts in ((rate_rows, rates), (pull_rows, pulls)):
            for block, value in enumerate(widen(*parts, lane)):
                ref[block, top : top + count, :] = value
        top += count
    for group in range(GROUPS):
        for ref, rows in ((rate, rate_rows), (pull, pull_rows)):
            for block in range(3):
                ref[group, :, block * 128 : (block + 1) * 128] = rows[block, pl.ds(group, 8, stride=GROUPS), :]

    for dy, dx in AROUND:

        @pl.when(inside(dy, dx) & (g >= 2))
        def _():
            arrival(patch_in.at[9 + slot(dy, dx)], patch_sem.at[9 + slot(dy, dx)])

        if (dy, dx) != (0, 0):

            @pl.when(inside(dy, dx))
            def _():
                arrival(patch_in.at[slot(dy, dx)], patch_sem.at[slot(dy, dx)])

    lane8 = iota((8, NODES), 1)
    bands = []
    for dy in (-1, 0, 1):
        parts = []
        for dx in (-1, 0, 1):
            tile = patch_in[slot(dy, dx)] + patch_in[9 + slot(dy, dx)]
            parts.append((tile, pltpu.roll(tile, 4, 0)))
        bands.append(jnp.concatenate(widen(*parts, lane8), axis=1))
    bands.append(jnp.zeros((8, LANES), f32))
    patch_rows = jnp.concatenate(bands, axis=0)
    high = patch_rows.astype(bf16)
    rest = patch_rows - high.astype(f32)
    middle = rest.astype(bf16)
    low = (rest - middle.astype(f32)).astype(bf16)
    target = mm(spread_rows[...], jnp.concatenate([high, middle, low, jnp.zeros_like(low)], axis=0))
    for group in range(GROUPS):
        value = target[group * 8 : (group + 1) * 8]
        mesh_a[group] = value
        pull[group] = pull[group] * value

    def sweep(src, dst):
        for group in range(GROUPS):
            here = src[group]
            above = pltpu.roll(src[GROUPS - 1], 1, 0) if group == 0 else src[group - 1]
            below = pltpu.roll(src[0], 7, 0) if group == GROUPS - 1 else src[group + 1]
            beside = pltpu.roll(here, 1, 1) + pltpu.roll(here, LANES - 1, 1)
            dst[group] = ((above + below) + beside) * rate[group] + pull[group]

    def two_sweeps(_, carry):
        sweep(mesh_a, mesh_b)
        sweep(mesh_b, mesh_a)
        return carry

    lax.fori_loop(0, SWEEPS // 2, two_sweeps, 0)

    for group in range(GROUPS):
        value = mesh_a[group]
        turned = [pltpu.roll(value[:, b * 128 : (b + 1) * 128], 64, 1) for b in (1, 2)]
        at = pl.ds(group, 8, stride=GROUPS)
        natural[0, at, :] = value[:, :128]
        natural[1, at, :] = jnp.where(lane8 < 64, turned[0], turned[1])
    rows = natural[0, SWEEPS : SWEEPS + NODES, :]
    cols = natural[1, SWEEPS : SWEEPS + NODES, :]
    mesh_out[0, 0] = rows
    mesh_out[0, 1] = cols

    sub_i, lane_i = iota((NODES, NODES), 0), iota((NODES, NODES), 1)
    sub_f, lane_f = sub_i.astype(f32), lane_i.astype(f32)
    eye = sub_i == lane_i
    to_row = lambda col: jnp.sum(jnp.where(eye, col, 0.0), axis=0, keepdims=True)
    to_col = lambda row: jnp.sum(jnp.where(eye, row, 0.0), axis=1, keepdims=True)
    land = lambda at: jnp.clip(at, 0.0, NODES - 1.0)
    col_0 = land(sub_f[:, :1] + jnp.sum(rows, axis=1, keepdims=True) / NODES)
    row_1 = land(lane_f[:1] + jnp.sum(cols, axis=0, keepdims=True) / NODES)
    row_0 = to_row(col_0)
    sub16 = iota((16, NODES), 0)
    land_out[...] = jnp.where(sub16 == 0, row_0, jnp.where(sub16 == 1, row_1, 0.0))

    def land_copy(step):
        return remote(
            land_out, land_in.at[g], land_sent.at[step - 1], land_sem.at[g], (g + step, y, x)
        )

    for step in range(1, n_gz):

        @pl.when(g + step < n_gz)
        def _():
            land_copy(step).start()

    col_1 = to_col(row_1)
    for t in range(n_gz - 1):

        @pl.when(t < g)
        def _():
            arrival(land_in.at[t], land_sem.at[t])

    for c, column in ((0, col_0), (1, col_1)):
        value = column
        for t in range(n_gz - 2, -1, -1):
            place = land_in[t, c : c + 1, :]
            if (n_gz - 2 - t) % 2 == 0:
                value = jnp.sum(hat(place - sub_f) * value, axis=0, keepdims=True)
            else:
                value = jnp.sum(hat(to_col(place) - lane_f) * value, axis=1, keepdims=True)
        if n_gz % 2:
            value = to_row(value)
        drift_out[0, 0, 0, c : c + 1, :] = value - lane_f[:1]

    for r in range(PER):

        @pl.when(g < n_gz - 1)
        def _():
            to_later(r).wait_send()

        @pl.when(g > 0)
        def _():
            to_earlier(r).wait_send()

    for dy, dx in AROUND:
        if (dy, dx) != (0, 0):

            @pl.when(inside(dy, dx))
            def _():
                anchor_copy(dy, dx).wait_send()
                patch_copy(0, dy, dx).wait_send()

        @pl.when(inside(dy, dx) & ahead)
        def _():
            patch_copy(1, dy, dx).wait_send()

    for step in range(1, n_gz):

        @pl.when(g + step < n_gz)
        def _():
            land_copy(step).wait_send()


def solution(mesh):
    sizes = tuple(mesh.shape[name] for name in ("gz", "ty", "tx"))
    n_gz = sizes[0]
    constants = tables()
    dma = pltpu.SemaphoreType.DMA

    def local(images, boundary, anchor):
        vmem = pl.BlockSpec(memory_space=pltpu.VMEM)
        hbm = pl.BlockSpec(memory_space=pl.ANY)
        return pl.pallas_call(
            functools.partial(kernel, sizes),
            out_shape=(
                jax.ShapeDtypeStruct((1, 2, NODES, NODES), f32),
                jax.ShapeDtypeStruct((1, 1, 1, 2, NODES), f32),
            ),
            in_specs=[hbm] * 3 + [vmem] * len(constants),
            out_specs=(vmem, vmem),
            scratch_shapes=[
                pltpu.VMEM((PER, PATCH, TILE), bf16),
                pltpu.VMEM((PER, PATCH, TILE), bf16),
                pltpu.VMEM((PER, PATCH, TILE), bf16),
                pltpu.VMEM((9, NODES, NODES), f32),
                pltpu.VMEM((18, 8, NODES), f32),
                pltpu.VMEM((2, 8, NODES), f32),
                pltpu.VMEM((2, 2, PER * PER, PATCH), f32),
                pltpu.VMEM((n_gz, 16, NODES), f32),
                pltpu.VMEM((16, NODES), f32),
                pltpu.VMEM((3, WIDE, 128), f32),
                pltpu.VMEM((3, WIDE, 128), f32),
                pltpu.VMEM((GROUPS, 8, LANES), f32),
                pltpu.VMEM((GROUPS, 8, LANES), f32),
                pltpu.VMEM((GROUPS, 8, LANES), f32),
                pltpu.VMEM((GROUPS, 8, LANES), f32),
                pltpu.VMEM((2, WIDE, NODES), f32),
                dma((PER,)),
                dma((PER,)),
                dma((PER,)),
                dma((PER,)),
                dma((PER,)),
                dma((9,)),
                dma((9,)),
                dma,
                dma((18,)),
                dma((18,)),
                dma((n_gz,)),
                dma((n_gz,)),
            ],
            compiler_params=pltpu.CompilerParams(
                collective_id=0, has_side_effects=True, vmem_limit_bytes=48 * 1024 * 1024
            ),
            name="align",
        )(images, boundary, anchor, *(jnp.asarray(c) for c in constants))

    return jax.shard_map(
        local,
        mesh=mesh,
        in_specs=(P("gz", "ty", "tx"), P("ty", "tx"), P("gz", "ty", "tx")),
        out_specs=(P("gz", None, "ty", "tx"), P("gz", "ty", "tx", None, None)),
        check_vma=False,
    )
```

profile of v0, /device:TPU:70, one launch (start us, length us, event | category | flops | bytes accessed | tf_op | source)
XLA Modules:
  0.0 44.6 jit_solution(3139804769604079021)
XLA Ops:
  0.6 0.0 copy-start.9
  0.6 0.7 %copy-done.9 = f32[16,128]{1,0:T(8,128)S(1)} copy-done((f32[16,128]{1,0:T(8,128)S(1)}, f32[16,128]{1,0:T(8,128)}, u32[]{:S(2)}) %copy-start.9) | copy-done | bytes 8216
  1.3 0.0 copy-start
  1.3 1.0 %copy-done = bf16[1,512,512]{2,1,0:T(8,128)(2,1)S(1)} copy-done((bf16[1,512,512]{2,1,0:T(8,128)(2,1)S(1)}, bf16[1,512,512]{2,1,0:T(8,128)(2,1)}, u32[]{:S(2)}) %copy-start) | copy-done | bytes 524312
  2.4 0.0 copy-start.1
  2.4 1.0 %copy-done.1 = bf16[512,512]{1,0:T(8,128)(2,1)S(1)} copy-done((bf16[512,512]{1,0:T(8,128)(2,1)S(1)}, bf16[512,512]{1,0:T(8,128)(2,1)}, u32[]{:S(2)}) %copy-start.1) | copy-done | bytes 524312
  3.4 0.0 copy-start.2
  3.4 0.9 %copy-done.2 = bf16[256,512]{1,0:T(8,128)(2,1)S(1)} copy-done((bf16[256,512]{1,0:T(8,128)(2,1)S(1)}, bf16[256,512]{1,0:T(8,128)(2,1)}, u32[]{:S(2)}) %copy-start.2) | copy-done | bytes 262168
  4.4 0.0 copy-start.3
  4.4 0.9 %copy-done.3 = bf16[256,256]{1,0:T(8,128)(2,1)S(1)} copy-done((bf16[256,256]{1,0:T(8,128)(2,1)S(1)}, bf16[256,256]{1,0:T(8,128)(2,1)}, u32[]{:S(2)}) %copy-start.3) | copy-done | bytes 131096
  5.3 0.0 copy-start.4
  5.3 0.9 %copy-done.4 = bf16[256,256]{1,0:T(8,128)(2,1)S(1)} copy-done((bf16[256,256]{1,0:T(8,128)(2,1)S(1)}, bf16[256,256]{1,0:T(8,128)(2,1)}, u32[]{:S(2)}) %copy-start.4) | copy-done | bytes 131096
  6.2 0.0 copy-start.5
  6.2 0.9 %copy-done.5 = bf16[256,256]{1,0:T(8,128)(2,1)S(1)} copy-done((bf16[256,256]{1,0:T(8,128)(2,1)S(1)}, bf16[256,256]{1,0:T(8,128)(2,1)}, u32[]{:S(2)}) %copy-start.5) | copy-done | bytes 131096
  7.1 0.0 copy-start.6
  7.1 0.8 %copy-done.6 = f32[1,128,128]{2,1,0:T(8,128)S(1)} copy-done((f32[1,128,128]{2,1,0:T(8,128)S(1)}, f32[1,128,128]{2,1,0:T(8,128)}, u32[]{:S(2)}) %copy-start.6) | copy-done | bytes 65560
  7.9 0.0 copy-start.7
  7.9 0.8 %copy-done.7 = bf16[256,128]{1,0:T(8,128)(2,1)S(1)} copy-done((bf16[256,128]{1,0:T(8,128)(2,1)S(1)}, bf16[256,128]{1,0:T(8,128)(2,1)}, u32[]{:S(2)}) %copy-start.7) | copy-done | bytes 65560
  8.8 0.0 copy-start.8
  8.8 0.8 %copy-done.8 = bf16[192,128]{1,0:T(8,128)(2,1)S(1)} copy-done((bf16[192,128]{1,0:T(8,128)(2,1)S(1)}, bf16[192,128]{1,0:T(8,128)(2,1)}, u32[]{:S(2)}) %copy-start.8) | copy-done | bytes 49176
  9.6 33.8 %align.1 = (f32[1,2,128,128]{3,2,1,0:T(8,128)S(1)}, f32[1,1,1,2,128]{4,3,2,1,0:T(2,128)S(1)}) custom-call(bf16[1,512,512]{2,1,0:T(8,128)(2,1)S(1)} %copy-done, bf16[512,512]{1,0:T(8,128)(2,1)S(1)} %copy-done.1, f32[1,128,128]{2,1,0:T(8,128)S(1)} %copy-done.6, bf16[256,128]{1,0:T(8,128)(2,1)S(1)} %copy-done.7, bf16[256,256]{1,0:T(8,128)(2,1)S(1)} %copy-done.5, ...), custom_call_target="tpu_custom_call" | custom-call | tf_op jit(solution)/shard_map/align/pallas_call | solution.py:533
  43.4 0.7 %copy.14 = f32[1,2,128,128]{3,2,1,0:T(8,128)} copy(f32[1,2,128,128]{3,2,1,0:T(8,128)S(1)} %get-tuple-element.4) | data formatting | bytes 262144
  44.1 0.6 %copy.15 = f32[1,1,1,2,128]{4,3,2,1,0:T(2,128)} copy(f32[1,1,1,2,128]{4,3,2,1,0:T(2,128)S(1)} %get-tuple-element.5) | data formatting | bytes 2048
Async XLA Ops:
  0.6 0.7 %copy-start.9 = (f32[16,128]{1,0:T(8,128)S(1)}, f32[16,128]{1,0:T(8,128)}, u32[]{:S(2)}) copy-start(f32[16,128]{1,0:T(8,128)} %constant.19.clone.spread_lanes) | copy-start | bytes 24580
  1.3 1.0 %copy-start = (bf16[1,512,512]{2,1,0:T(8,128)(2,1)S(1)}, bf16[1,512,512]{2,1,0:T(8,128)(2,1)}, u32[]{:S(2)}) copy-start(bf16[1,512,512]{2,1,0:T(8,128)(2,1)} %images.1) | copy-start | bytes 1572868
  2.4 1.0 %copy-start.1 = (bf16[512,512]{1,0:T(8,128)(2,1)S(1)}, bf16[512,512]{1,0:T(8,128)(2,1)}, u32[]{:S(2)}) copy-start(bf16[512,512]{1,0:T(8,128)(2,1)} %boundary.1) | copy-start | bytes 1572868
  3.4 0.9 %copy-start.2 = (bf16[256,512]{1,0:T(8,128)(2,1)S(1)}, bf16[256,512]{1,0:T(8,128)(2,1)}, u32[]{:S(2)}) copy-start(bf16[256,512]{1,0:T(8,128)(2,1)} %constant.16.clone.right_pair) | copy-start | bytes 786436
  4.4 0.9 %copy-start.3 = (bf16[256,256]{1,0:T(8,128)(2,1)S(1)}, bf16[256,256]{1,0:T(8,128)(2,1)}, u32[]{:S(2)}) copy-start(bf16[256,256]{1,0:T(8,128)(2,1)} %constant.18.clone.back_left) | copy-start | bytes 393220
  5.3 0.9 %copy-start.4 = (bf16[256,256]{1,0:T(8,128)(2,1)S(1)}, bf16[256,256]{1,0:T(8,128)(2,1)}, u32[]{:S(2)}) copy-start(bf16[256,256]{1,0:T(8,128)(2,1)} %constant.17.clone.back_right) | copy-start | bytes 393220
  6.2 0.9 %copy-start.5 = (bf16[256,256]{1,0:T(8,128)(2,1)S(1)}, bf16[256,256]{1,0:T(8,128)(2,1)}, u32[]{:S(2)}) copy-start(bf16[256,256]{1,0:T(8,128)(2,1)} %constant.15.clone.right) | copy-start | bytes 393220
  7.1 0.8 %copy-start.6 = (f32[1,128,128]{2,1,0:T(8,128)S(1)}, f32[1,128,128]{2,1,0:T(8,128)}, u32[]{:S(2)}) copy-start(f32[1,128,128]{2,1,0:T(8,128)} %anchor.1) | copy-start | bytes 196612
  7.9 0.8 %copy-start.7 = (bf16[256,128]{1,0:T(8,128)(2,1)S(1)}, bf16[256,128]{1,0:T(8,128)(2,1)}, u32[]{:S(2)}) copy-start(bf16[256,128]{1,0:T(8,128)(2,1)} %constant.14.clone.left) | copy-start | bytes 196612
  8.8 0.8 %copy-start.8 = (bf16[192,128]{1,0:T(8,128)(2,1)S(1)}, bf16[192,128]{1,0:T(8,128)(2,1)}, u32[]{:S(2)}) copy-start(bf16[192,128]{1,0:T(8,128)(2,1)} %constant.20.clone.spread_rows) | copy-start | bytes 147460
where the time goes:
time: 45.4 us; the launch traced here: 44.6 us
  Pallas kernels  33.8 us (74%)
  local copies, waits for them, and re-layouts  10.1 us (22%)
  between operations  0.66 us (1%)
    pallas_call x1, Pallas kernels, local(): pl.pallas_call(functools.partial(kernel, sizes), out_shape=(jax.ShapeDtyp...  33.8 us
    unnamed x22, local copies, waits for them, and re-layouts  10.1 us

commit v1 on v0

v1 whole, which is shorter than its diff:
```python
import functools
import math

import jax
import jax.numpy as jnp
import numpy as np
from jax import lax
from jax.experimental import pallas as pl
from jax.experimental.pallas import tpu as pltpu
from jax.sharding import PartitionSpec as P

PATCH = 128
STRIDE = 4
SWEEPS = 32
TILE = 512
NODES = 128
PER = TILE // PATCH
WIDE = NODES + 2 * SWEEPS
GROUPS = WIDE // 8
LANES = 2 * WIDE

GRANT = 48 * 1024 * 1024

f32 = jnp.float32
bf16 = jnp.bfloat16
MESH = pl.DeviceIdType.MESH
AROUND = [(dy, dx) for dy in (-1, 0, 1) for dx in (-1, 0, 1)]


def slot(dy, dx):
    return (dy + 1) * 3 + dx + 1


def pieces(table, count):
    parts = []
    rest = np.asarray(table, np.float64)
    for _ in range(count):
        part = rest.astype(jnp.bfloat16)
        parts.append(part)
        rest = rest - part.astype(np.float64)
    return parts


def spread_table():
    pos = (np.arange(NODES) + 0.5) * STRIDE / PATCH - 0.5
    weights = np.maximum(0.0, 1.0 - np.abs(pos[:, None] - np.arange(PER)[None, :]))
    return weights / weights.sum(axis=1, keepdims=True)


def tables():
    half = PATCH // 2
    n = np.arange(PATCH)
    angle = lambda k: 2.0 * np.pi * (n[:, None] * k[None, :] % PATCH) / PATCH
    low, high = np.arange(half), np.arange(1, half)
    cos_low, sin_high = np.cos(angle(low)), np.sin(angle(high))
    last = np.cos(np.pi * n)[:, None]
    zero = np.zeros_like(last)
    basis = np.concatenate([cos_low, last, sin_high], axis=1)
    same = np.concatenate([cos_low, last, cos_low[:, 1:]], axis=1)
    cross = np.concatenate([zero, sin_high, zero, -sin_high], axis=1)
    weight = np.full(PATCH, 2.0 / PATCH)
    weight[[0, half]] = 1.0 / PATCH
    inverse = basis * weight[None, :]

    b_hi, b_lo = pieces(basis, 2)
    s_hi, s_lo = pieces(same, 2)
    c_hi, c_lo = pieces(cross, 2)
    r_hi, r_lo = pieces(inverse.T, 2)
    l_hi, l_lo = pieces(inverse * (math.log2(math.e) / PATCH), 2)
    left = np.concatenate([b_hi.T, b_lo.T], axis=0)
    right = np.concatenate([b_hi, b_lo], axis=1)
    right_pair = np.concatenate([s_hi, c_hi, s_lo, c_lo], axis=1)
    back_right = np.concatenate([r_hi, r_lo], axis=1)
    back_left = np.concatenate([l_hi, l_lo], axis=0)
    twice = lambda t, axis: np.concatenate([t, t], axis=axis)

    spread = spread_table()
    rows = np.zeros((WIDE, 128))
    for group in range(GROUPS):
        for sub in range(8):
            i = sub * GROUPS + group - SWEEPS
            dy = i // NODES
            for piece in range(3):
                first = piece * 32 + (dy + 1) * 8
                rows[group * 8 + sub, first : first + PER] = spread[i - dy * NODES]
    cols = np.zeros((128, LANES))
    take = np.zeros((256, LANES))
    give = np.zeros((LANES, 2 * NODES))
    for u in range(3):
        for lane in range(128):
            comp, j = lane // 64, lane % 64 * 3 + u - SWEEPS
            dx = j // NODES
            at = u * 128 + lane
            for piece in range(3):
                first = piece * 32 + (dx + 1) * 8 + comp * PER
                cols[first : first + PER, at] = spread[j - dx * NODES]
            take[j if dx == 0 else 128 + j % NODES, at] = 1.0
            if dx == 0:
                give[at, comp * NODES + j] = 1.0
    return tuple(
        t.astype(jnp.bfloat16)
        for t in (
            left,
            twice(right, 0),
            twice(right_pair, 0),
            twice(back_right, 0),
            twice(back_left, 1),
            take,
            cols,
            rows,
            give,
        )
    )


def mm(a, b):
    return jnp.dot(a, b, preferred_element_type=f32)


def halves(value):
    hi = value.astype(bf16)
    return hi, (value - hi.astype(f32)).astype(bf16)


def iota(shape, dim):
    return lax.broadcasted_iota(jnp.int32, shape, dim)


def stacked_rows(wide):
    return jnp.concatenate([wide[:, q * PATCH : (q + 1) * PATCH] for q in range(PER)], axis=0)


def side_by_side(tall):
    return jnp.concatenate([tall[q * PATCH : (q + 1) * PATCH] for q in range(PER)], axis=1)


def row_pass(pixels, left):
    both = mm(left[...], pixels)
    return jnp.concatenate(halves(stacked_rows(both[:PATCH] + both[PATCH:])), axis=1)


def packed_spectrum(pixels, left, right):
    both = mm(row_pass(pixels, left), right[...])
    return both[:, :PATCH] + both[:, PATCH:]


def paired_spectrum(pixels, left, right_pair):
    both = mm(row_pass(pixels, left), right_pair[...])
    return (
        both[:, :PATCH] + both[:, 2 * PATCH : 3 * PATCH],
        both[:, PATCH : 2 * PATCH] + both[:, 3 * PATCH :],
    )


def cross_spectrum(pair, later):
    half = PATCH // 2
    same, cross = pair
    turned = pltpu.roll(later, half, 1)
    first = iota((half, PATCH), 0) == 0
    out = []
    for q in range(PER):
        top = slice(q * PATCH, q * PATCH + half)
        low = slice(q * PATCH + half, (q + 1) * PATCH)
        joint = lambda e, c: same[e] * later[c] + cross[e] * turned[c]
        low_low = joint(low, low)
        out.append(joint(top, top) + jnp.where(first, 0.0, low_low))
        out.append(jnp.where(first, low_low, joint(top, low) - joint(low, top)))
    return jnp.concatenate(out, axis=0)


def scores(product, back_right, back_left):
    both = mm(jnp.concatenate(halves(product), axis=1), back_right[...])
    wide = side_by_side(both[:, :PATCH] + both[:, PATCH:])
    both = mm(back_left[...], jnp.concatenate(halves(wide), axis=0))
    return both[:PATCH] + both[PATCH:]


def signed_lag(shape, dim):
    lag = iota(shape, dim)
    return jnp.where(lag < PATCH // 2, lag, lag - PATCH).astype(f32)


def hat(offset):
    return jnp.maximum(0.0, 1.0 - jnp.abs(offset))


def thirds(value):
    high = value.astype(bf16)
    rest = value - high.astype(f32)
    middle = rest.astype(bf16)
    return high, middle, (rest - middle.astype(f32)).astype(bf16)


def moved(value, selection):
    count = value.shape[0]
    parts = mm(jnp.concatenate(thirds(value), axis=0), selection)
    return parts[:count] + parts[count : 2 * count] + parts[2 * count :]


def kernel(
    sizes,
    images, boundary, anchor, *rest,
):
    n_gz, n_ty, n_tx = sizes
    tables_in, rest = rest[:9], rest[9:]
    (
        mesh_out, land_all,
        own, before, after, spectra, ties, patch_in, patch_out, sums, land_in, land_out,
        rate, pull, mesh_a, mesh_b,
    ) = rest[:16]
    tables_here, rest = rest[16:25], rest[25:]
    (
        table_sem, own_sem, before_sem, after_sem, up_sem, down_sem, tie_sem, tie_sent,
        patch_sem, patch_sent, land_sem, land_sent,
    ) = rest
    left, right, right_pair, back_right, back_left, take, spread_cols, spread_rows, give = tables_here
    g, y, x = lax.axis_index("gz"), lax.axis_index("ty"), lax.axis_index("tx")

    def inside(dy, dx):
        ok = None
        for pos, step, count in ((y, dy, n_ty), (x, dx, n_tx)):
            if step:
                here = (pos + step >= 0) & (pos + step < count)
                ok = here if ok is None else ok & here
        return (g >= 0) if ok is None else ok

    barrier = pltpu.get_barrier_semaphore()
    greeted = jnp.int32(0)

    def greet(ok, device):
        @pl.when(ok)
        def _():
            pl.semaphore_signal(barrier, inc=1, device_id=device, device_id_type=MESH)

        return jnp.where(ok, 1, 0).astype(jnp.int32)

    for step in range(2, n_gz):
        greeted += greet(g + step < n_gz, (g + step, y, x))
        greeted += greet(g - step >= 0, (g - step, y, x))
    for dz in (-1, 1, 0):
        for dy, dx in AROUND:
            if (dz, dy, dx) != (0, 0, 0):
                ok = inside(dy, dx) & (g + dz >= 0) & (g + dz < n_gz)
                greeted += greet(ok, (g + dz, y + dy, x + dx))

    def band(ref, r):
        return ref.at[pl.ds(pl.multiple_of(r * PATCH, PATCH), PATCH), :]

    table_copies = [
        pltpu.make_async_copy(src, dst, table_sem.at[i])
        for i, (src, dst) in enumerate(zip(tables_in, tables_here))
    ]
    for copy in table_copies[:2]:
        copy.start()
    for r in range(PER):
        pltpu.make_async_copy(band(images.at[0], r), own.at[r], own_sem.at[r]).start()
    for copy in table_copies[2:]:
        copy.start()
    tie_own = pltpu.make_async_copy(
        anchor.at[0], ties.at[1, pl.ds(SWEEPS, NODES), :], tie_sem.at[slot(0, 0)]
    )
    tie_own.start()
    for r in range(PER):

        @pl.when(g == 0)
        def _():
            pltpu.make_async_copy(band(boundary, r), before.at[r], before_sem.at[r]).start()

        @pl.when(g == n_gz - 1)
        def _():
            pltpu.make_async_copy(band(boundary, r), after.at[r], after_sem.at[r]).start()

    ramp_rows = iota((8, NODES), 1).astype(f32)
    for t in range(n_gz):

        @pl.when(t >= g)
        def _():
            land_in[t] = ramp_rows

    for edge, count, first in ((y == 0, SWEEPS, 0), (y == n_ty - 1, SWEEPS, SWEEPS + NODES)):

        @pl.when(edge)
        def _():
            for d in range(3):
                ties[d, pl.ds(first, count), :] = jnp.zeros((count, NODES), f32)

    for edge, d in ((x == 0, 0), (x == n_tx - 1, 2)):

        @pl.when(edge)
        def _():
            ties[d] = jnp.zeros((WIDE, NODES), f32)

    for dy, dx in AROUND:
        if (dy, dx) != (0, 0):

            @pl.when(jnp.logical_not(inside(dy, dx)))
            def _():
                patch_in[slot(dy, dx)] = jnp.zeros((8, NODES), f32)

        @pl.when(jnp.logical_not(inside(dy, dx)) | (g < 2))
        def _():
            patch_in[9 + slot(dy, dx)] = jnp.zeros((8, NODES), f32)

    pl.semaphore_wait(barrier, greeted)

    def remote(src, dst, sent, arrived, device):
        return pltpu.make_async_remote_copy(
            src_ref=src, dst_ref=dst, send_sem=sent, recv_sem=arrived, device_id=device, device_id_type=MESH
        )

    def to_later(r):
        return remote(band(images.at[0], r), before.at[r], up_sem.at[r], before_sem.at[r], (g + 1, y, x))

    def to_earlier(r):
        return remote(band(images.at[0], r), after.at[r], down_sem.at[r], after_sem.at[r], (g - 1, y, x))

    for r in range(PER):

        @pl.when(g < n_gz - 1)
        def _():
            to_later(r).start()

        @pl.when(g > 0)
        def _():
            to_earlier(r).start()

    rows_of = {-1: (0, SWEEPS), 0: (0, NODES), 1: (NODES - SWEEPS, SWEEPS)}
    place_of = {-1: 0, 0: SWEEPS, 1: SWEEPS + NODES}

    def tie_copy(dy, dx):
        first, count = rows_of[dy]
        to = slot(-dy, -dx)
        return remote(
            anchor.at[0, pl.ds(first, count), :],
            ties.at[1 - dx, pl.ds(place_of[-dy], count), :],
            tie_sent.at[to],
            tie_sem.at[to],
            (g, y + dy, x + dx),
        )

    for dy, dx in AROUND:
        if (dy, dx) != (0, 0):

            @pl.when(inside(dy, dx))
            def _():
                tie_copy(dy, dx).start()

    def arrival(ref, sem):
        pltpu.make_async_copy(ref, ref, sem).wait()

    for copy in table_copies[:2]:
        copy.wait()

    def own_step(r, carry):
        arrival(own.at[r], own_sem.at[r])
        spectra[r] = packed_spectrum(own[r], left, right)
        return carry

    lax.fori_loop(0, PER, own_step, 0)

    for copy in table_copies[2:]:
        copy.wait()
    tie_own.wait()
    for dy, dx in AROUND:
        if (dy, dx) != (0, 0):
            first, count = rows_of[-dy]
            part = ties.at[dx + 1, pl.ds(place_of[dy], count), :]

            @pl.when(inside(dy, dx))
            def _():
                arrival(part, tie_sem.at[slot(dy, dx)])

    lane8, sub8 = iota((8, 128), 1), iota((8, 128), 0)

    def limits(pos, count):
        return jnp.where(pos == 0, 0, -SWEEPS), jnp.where(pos == count - 1, NODES, NODES + SWEEPS)

    row_first, row_last = limits(y, n_ty)
    col_first, col_last = limits(x, n_tx)
    picked = []
    for group in range(GROUPS):
        at = pl.ds(group, 8, stride=GROUPS)
        picked.append(jnp.concatenate([ties[1, at, :], jnp.where(lane8 < 64, ties[2, at, :], ties[0, at, :])], axis=1))
    tie = moved(jnp.concatenate(picked, axis=0), take[...])
    for group in range(GROUPS):
        i = sub8 * GROUPS + (group - SWEEPS)
        for u in range(3):
            j = lane8 % 64 * 3 + (u - SWEEPS)
            kept = (i >= row_first) & (i < row_last) & (j >= col_first) & (j < col_last)
            value = tie[group * 8 : (group + 1) * 8, u * 128 : (u + 1) * 128]
            held = jnp.where(kept, 1.0 / (4.0 + value), 0.0)
            rate[group, :, u * 128 : (u + 1) * 128] = held
            pull[group, :, u * 128 : (u + 1) * 128] = value * held

    lag_rows = signed_lag((PATCH, PATCH), 0)

    def softmax_sums(wide, pair, r):
        for q in range(PER):
            score = wide[:, q * PATCH : (q + 1) * PATCH]
            weight = jnp.exp2(score - jnp.max(score))
            at = pl.ds(q * PER + r, 1)
            sums[pair, 0, at, :] = jnp.sum(weight, axis=0, keepdims=True)
            sums[pair, 1, at, :] = jnp.sum(weight * lag_rows, axis=0, keepdims=True)

    def band_step(r, carry):
        arrival(before.at[r], before_sem.at[r])
        arrival(after.at[r], after_sem.at[r])
        pair = paired_spectrum(before[r], left, right_pair)
        there = packed_spectrum(after[r], left, right)
        near = scores(cross_spectrum(pair, spectra[r]), back_right, back_left)
        far = scores(cross_spectrum(pair, there), back_right, back_left)
        softmax_sums(near, 0, r)
        softmax_sums(far, 1, r)
        return carry

    lax.fori_loop(0, PER, band_step, 0)

    lag_lanes = signed_lag((PER * PER, PATCH), 1)
    col_of = iota((PER * PER, 128), 1) - iota((PER * PER, 128), 0) // PER

    def flow(pair):
        weight = sums[pair, 0]
        scale = (1.0 / STRIDE) / jnp.sum(weight, axis=1, keepdims=True)
        rows = jnp.sum(sums[pair, 1], axis=1, keepdims=True) * scale
        cols = jnp.sum(weight * lag_lanes, axis=1, keepdims=True) * scale
        return rows, cols

    def patch_tile(rows, cols):
        part = jnp.where(col_of == 0, rows, jnp.where(col_of == PER, cols, 0.0))
        part = part[:8] + part[8:]
        return part + pltpu.roll(part, 4, 0)

    near, far = flow(0), flow(1)
    near_scale = jnp.where(g >= 2, 0.5, 1.0).astype(f32)
    for kind, flows in ((1, [0.5 * (b - a) for a, b in zip(near, far)]), (0, [near_scale * v for v in near])):
        tile = patch_tile(*flows)
        for d in range(3):
            value = tile if d == 0 else pltpu.roll(tile, 8 * d, 1)
            patch_out[kind, d] = value
            if (kind, d) == (0, 1):
                patch_in[slot(0, 0)] = value

    def patch_copy(kind, dy, dx):
        to = 9 * kind + slot(-dy, -dx)
        return remote(
            patch_out.at[kind, 1 - dx], patch_in.at[to], patch_sent.at[to], patch_sem.at[to],
            (g + kind, y + dy, x + dx),
        )

    ahead = (g >= 1) & (g < n_gz - 1)
    for dy, dx in sorted(AROUND, key=lambda d: -abs(d[0]) - abs(d[1])):

        @pl.when(inside(dy, dx) & ahead)
        def _():
            patch_copy(1, dy, dx).start()

        if (dy, dx) != (0, 0):

            @pl.when(inside(dy, dx))
            def _():
                patch_copy(0, dy, dx).start()

    for dy, dx in AROUND:

        @pl.when(inside(dy, dx) & (g >= 2))
        def _():
            arrival(patch_in.at[9 + slot(dy, dx)], patch_sem.at[9 + slot(dy, dx)])

        if (dy, dx) != (0, 0):

            @pl.when(inside(dy, dx))
            def _():
                arrival(patch_in.at[slot(dy, dx)], patch_sem.at[slot(dy, dx)])

    bands = []
    for dy in (-1, 0, 1):
        total = None
        for dx in (-1, 0, 1):
            tile = patch_in[slot(dy, dx)] + patch_in[9 + slot(dy, dx)]
            total = tile if total is None else total + tile
        bands.append(total)
    bands.append(jnp.zeros((8, 128), f32))
    high, middle, low = (v.astype(f32) for v in thirds(jnp.concatenate(bands, axis=0)))
    patches = (high + pltpu.roll(middle, 32, 1)) + pltpu.roll(low, 64, 1)
    parts = thirds(mm(patches.astype(bf16), spread_cols[...]))
    target = mm(spread_rows[...], jnp.concatenate([*parts, jnp.zeros_like(parts[0])], axis=0))
    for group in range(GROUPS):
        value = target[group * 8 : (group + 1) * 8]
        mesh_a[group] = value
        pull[group] = pull[group] * value

    def sweep(src, dst):
        for group in range(GROUPS):
            here = src[group]
            above = pltpu.roll(src[GROUPS - 1], 1, 0) if group == 0 else src[group - 1]
            below = pltpu.roll(src[0], 7, 0) if group == GROUPS - 1 else src[group + 1]
            first, second, third = (here[:, u * 128 : (u + 1) * 128] for u in range(3))
            beside = jnp.concatenate(
                [pltpu.roll(third, 1, 1) + second, first + third, second + pltpu.roll(first, 127, 1)], axis=1
            )
            dst[group] = ((above + below) + beside) * rate[group] + pull[group]

    def two_sweeps(_, carry):
        sweep(mesh_a, mesh_b)
        sweep(mesh_b, mesh_a)
        return carry

    lax.fori_loop(0, SWEEPS // 2, two_sweeps, 0)

    natural = ties
    ordered = moved(jnp.concatenate([mesh_a[group] for group in range(GROUPS)], axis=0), give[...])
    for group in range(GROUPS):
        at = pl.ds(group, 8, stride=GROUPS)
        for c in range(2):
            natural[c, at, :] = ordered[group * 8 : (group + 1) * 8, c * NODES : (c + 1) * NODES]
    rows = natural[0, SWEEPS : SWEEPS + NODES, :]
    cols = natural[1, SWEEPS : SWEEPS + NODES, :]
    land = lambda at: jnp.clip(at, 0.0, NODES - 1.0)
    sub_i, lane_i = iota((NODES, NODES), 0), iota((NODES, NODES), 1)
    col_0 = land(sub_i[:, :1].astype(f32) + jnp.sum(rows, axis=1, keepdims=True) / NODES)
    row_0 = jnp.sum(jnp.where(sub_i == lane_i, col_0, 0.0), axis=0, keepdims=True)
    row_1 = land(lane_i[:1].astype(f32) + jnp.sum(cols, axis=0, keepdims=True) / NODES)
    landing = jnp.where(sub8 == 0, row_0, jnp.where(sub8 == 1, row_1, 0.0))
    land_out[...] = landing

    def land_copy(step):
        return remote(
            land_out, land_in.at[g], land_sent.at[step - 1], land_sem.at[g], (g + step, y, x)
        )

    for step in range(n_gz - 1, 0, -1):

        @pl.when(g + step < n_gz)
        def _():
            land_copy(step).start()

    mesh_out[0] = rows
    mesh_out[1] = cols
    land_all[n_gz] = landing

    for r in range(PER):

        @pl.when(g < n_gz - 1)
        def _():
            to_later(r).wait_send()

        @pl.when(g > 0)
        def _():
            to_earlier(r).wait_send()

    for dy, dx in AROUND:
        if (dy, dx) != (0, 0):

            @pl.when(inside(dy, dx))
            def _():
                tie_copy(dy, dx).wait_send()
                patch_copy(0, dy, dx).wait_send()

        @pl.when(inside(dy, dx) & ahead)
        def _():
            patch_copy(1, dy, dx).wait_send()

    for t in range(n_gz - 1):

        @pl.when(t < g)
        def _():
            arrival(land_in.at[t], land_sem.at[t])

    for t in range(n_gz):
        land_all[t] = land_in[t]

    for step in range(1, n_gz):

        @pl.when(g + step < n_gz)
        def _():
            land_copy(step).wait_send()


def finish(n_gz, mesh_in, land_all, mesh_out, drift_out, sem):
    copy = pltpu.make_async_copy(mesh_in, mesh_out.at[0], sem)
    copy.start()
    sub_i, lane_i = iota((NODES, NODES), 0), iota((NODES, NODES), 1)
    sub_f, lane_f = sub_i.astype(f32), lane_i.astype(f32)
    eye = sub_i == lane_i
    to_row = lambda col: jnp.sum(jnp.where(eye, col, 0.0), axis=0, keepdims=True)
    to_col = lambda row: jnp.sum(jnp.where(eye, row, 0.0), axis=1, keepdims=True)
    for c in range(2):
        value = to_col(land_all[n_gz, c : c + 1, :])
        for t in range(n_gz - 2, -1, -1):
            place = land_all[t, c : c + 1, :]
            if (n_gz - 2 - t) % 2 == 0:
                value = jnp.sum(hat(place - sub_f) * value, axis=0, keepdims=True)
            else:
                value = jnp.sum(hat(to_col(place) - lane_f) * value, axis=1, keepdims=True)
        if n_gz % 2:
            value = to_row(value)
        drift_out[0, 0, 0, c : c + 1, :] = value - lane_f[:1]
    copy.wait()


def solution(mesh):
    sizes = tuple(mesh.shape[name] for name in ("gz", "ty", "tx"))
    n_gz = sizes[0]
    constants = tables()
    dma = pltpu.SemaphoreType.DMA
    vmem = pl.BlockSpec(memory_space=pltpu.VMEM)
    hbm = pl.BlockSpec(memory_space=pltpu.HBM)

    def local(images, boundary, anchor):
        relaxed, landings = pl.pallas_call(
            functools.partial(kernel, sizes),
            out_shape=(
                jax.ShapeDtypeStruct((2, NODES, NODES), f32),
                jax.ShapeDtypeStruct((n_gz + 1, 8, NODES), f32),
            ),
            in_specs=[hbm] * (3 + len(constants)),
            out_specs=(vmem, vmem),
            scratch_shapes=[
                pltpu.VMEM((PER, PATCH, TILE), bf16),
                pltpu.VMEM((PER, PATCH, TILE), bf16),
                pltpu.VMEM((PER, PATCH, TILE), bf16),
                pltpu.VMEM((PER, PER * PATCH, PATCH), f32),
                pltpu.VMEM((3, WIDE, NODES), f32),
                pltpu.VMEM((18, 8, NODES), f32),
                pltpu.VMEM((2, 3, 8, NODES), f32),
                pltpu.VMEM((2, 2, PER * PER, PATCH), f32),
                pltpu.VMEM((n_gz, 8, NODES), f32),
                pltpu.VMEM((8, NODES), f32),
                pltpu.VMEM((GROUPS, 8, LANES), f32),
                pltpu.VMEM((GROUPS, 8, LANES), f32),
                pltpu.VMEM((GROUPS, 8, LANES), f32),
                pltpu.VMEM((GROUPS, 8, LANES), f32),
                *(pltpu.VMEM(c.shape, bf16) for c in constants),
                dma((len(constants),)),
                dma((PER,)),
                dma((PER,)),
                dma((PER,)),
                dma((PER,)),
                dma((PER,)),
                dma((9,)),
                dma((9,)),
                dma((18,)),
                dma((18,)),
                dma((n_gz,)),
                dma((n_gz,)),
            ],
            compiler_params=pltpu.CompilerParams(
                collective_id=0, has_side_effects=True, vmem_limit_bytes=GRANT
            ),
            name="align",
        )(*(pltpu.with_memory_space_constraint(v, pltpu.HBM) for v in (images, boundary, anchor, *map(jnp.asarray, constants))))
        return pl.pallas_call(
            functools.partial(finish, n_gz),
            out_shape=(
                jax.ShapeDtypeStruct((1, 2, NODES, NODES), f32),
                jax.ShapeDtypeStruct((1, 1, 1, 2, NODES), f32),
            ),
            in_specs=[vmem, vmem],
            out_specs=(hbm, vmem),
            scratch_shapes=[dma],
            compiler_params=pltpu.CompilerParams(vmem_limit_bytes=4 * 1024 * 1024),
            name="finish",
        )(relaxed, landings)

    return jax.shard_map(
        local,
        mesh=mesh,
        in_specs=(P("gz", "ty", "tx"), P("ty", "tx"), P("gz", "ty", "tx")),
        out_specs=(P("gz", None, "ty", "tx"), P("gz", "ty", "tx", None, None)),
        check_vma=False,
    )
```

time: 45.4 us -> 29.4 us (0.65); the launches traced: 44.6 us -> 29.3 us
  local copies, waits for them, and re-layouts: 10.1 us -> 0 us
  Pallas kernels: 33.8 us -> 28.6 us
    unnamed x22 -> x0, local copies, waits for them, and re-layouts: 10.1 us -> none
    pallas_call x1, Pallas kernels: 33.8 us -> 27.4 us  [local(): pl.pallas_call(functools.partial(kernel, sizes), out_shape=(jax.ShapeDtyp...]
    pallas_call x0 -> x1, Pallas kernels: none -> 1.23 us  [local(): pl.pallas_call(functools.partial(finish, n_gz), out_shape=(jax.ShapeDtype...]
where the time goes in v1:
time: 29.4 us; the launch traced here: 29.3 us
  Pallas kernels  28.6 us (97%)
  between operations  0.64 us (2%)
    pallas_call x1, Pallas kernels, local(): pl.pallas_call(functools.partial(kernel, sizes), out_shape=(jax.ShapeDtyp...  27.4 us
    pallas_call x1, Pallas kernels, local(): pl.pallas_call(functools.partial(finish, n_gz), out_shape=(jax.ShapeDtype...  1.23 us

profile of v1, /device:TPU:70, one launch (start us, length us, event | category | flops | bytes accessed | tf_op | source)
XLA Modules:
  0.0 29.3 jit_solution(13365477465728608731)
XLA Ops:
  0.6 27.4 %align.1 = (f32[2,128,128]{2,1,0:T(8,128)S(1)}, f32[9,8,128]{2,1,0:T(8,128)S(1)}) custom-call(bf16[1,512,512]{2,1,0:T(8,128)(2,1)} %images.1, bf16[512,512]{1,0:T(8,128)(2,1)} %boundary.1, f32[1,128,128]{2,1,0:T(8,128)} %anchor.1, bf16[256,128]{1,0:T(8,128)(2,1)} %constant.18.clone.rest_0_, bf16[256,256]{1,0:T(8,128)(2,1)} %constant.19.clone.rest_1_, ...), custom_call_target="tpu_custom_call" | custom-call | tf_op jit(solution)/shard_map/align/pallas_call | solution.py:610
  28.0 1.2 %finish.1 = (f32[1,2,128,128]{3,2,1,0:T(8,128)}, f32[1,1,1,2,128]{4,3,2,1,0:T(2,128)}) custom-call(f32[2,128,128]{2,1,0:T(8,128)S(1)} %get-tuple-element.4.mesh_in, f32[9,8,128]{2,1,0:T(8,128)S(1)} %get-tuple-element.5.land_all), custom_call_target="tpu_custom_call" | custom-call | tf_op jit(solution)/shard_map/finish/pallas_call | solution.py:652

commit v2 on v1

--- a/solution.py
+++ b/solution.py
@@ -15,6 +15,9 @@
 TILE = 512
 NODES = 128
 PER = TILE // PATCH
+Q = 4
+WIDTH = Q * PATCH
+PIECES = PER * PER // Q
 WIDE = NODES + 2 * SWEEPS
 GROUPS = WIDE // 8
 LANES = 2 * WIDE
@@ -25,6 +28,8 @@
 bf16 = jnp.bfloat16
 MESH = pl.DeviceIdType.MESH
 AROUND = [(dy, dx) for dy in (-1, 0, 1) for dx in (-1, 0, 1)]
+SIDES = [(-1, 0), (1, 0), (0, -1), (0, 1)]
+CORNERS = [(-1, -1), (-1, 1), (1, -1), (1, 1)]
 
 
 def slot(dy, dx):
@@ -127,11 +132,11 @@
 
 
 def stacked_rows(wide):
-    return jnp.concatenate([wide[:, q * PATCH : (q + 1) * PATCH] for q in range(PER)], axis=0)
+    return jnp.concatenate([wide[:, q * PATCH : (q + 1) * PATCH] for q in range(wide.shape[1] // PATCH)], axis=0)
 
 
 def side_by_side(tall):
-    return jnp.concatenate([tall[q * PATCH : (q + 1) * PATCH] for q in range(PER)], axis=1)
+    return jnp.concatenate([tall[q * PATCH : (q + 1) * PATCH] for q in range(tall.shape[0] // PATCH)], axis=1)
 
 
 def row_pass(pixels, left):
@@ -158,7 +163,7 @@
     turned = pltpu.roll(later, half, 1)
     first = iota((half, PATCH), 0) == 0
     out = []
-    for q in range(PER):
+    for q in range(Q):
         top = slice(q * PATCH, q * PATCH + half)
         low = slice(q * PATCH + half, (q + 1) * PATCH)
         joint = lambda e, c: same[e] * later[c] + cross[e] * turned[c]
@@ -211,7 +216,7 @@
     tables_here, rest = rest[16:25], rest[25:]
     (
         table_sem, own_sem, before_sem, after_sem, up_sem, down_sem, tie_sem, tie_sent,
-        patch_sem, patch_sent, land_sem, land_sent,
+        patch_sem, patch_sent, land_sem, land_sent, rounds,
     ) = rest
     left, right, right_pair, back_right, back_left, take, spread_cols, spread_rows, give = tables_here
     g, y, x = lax.axis_index("gz"), lax.axis_index("ty"), lax.axis_index("tx")
@@ -224,27 +229,27 @@
                 ok = here if ok is None else ok & here
         return (g >= 0) if ok is None else ok
 
+    def told(semaphore, ok, device):
+        @pl.when(ok)
+        def _():
+            pl.semaphore_signal(semaphore, inc=1, device_id=device, device_id_type=MESH)
+
+        return jnp.where(ok, 1, 0).astype(jnp.int32)
+
+    def within(step):
+        return (g + step >= 0) & (g + step < n_gz)
+
+    near = [(within(dz), (g + dz, y, x)) for dz in (-1, 1)]
+    near += [(inside(dy, dx), (g, y + dy, x + dx)) for dy, dx in SIDES]
+
     barrier = pltpu.get_barrier_semaphore()
     greeted = jnp.int32(0)
-
-    def greet(ok, device):
-        @pl.when(ok)
-        def _():
-            pl.semaphore_signal(barrier, inc=1, device_id=device, device_id_type=MESH)
-
-        return jnp.where(ok, 1, 0).astype(jnp.int32)
-
-    for step in range(2, n_gz):
-        greeted += greet(g + step < n_gz, (g + step, y, x))
-        greeted += greet(g - step >= 0, (g - step, y, x))
-    for dz in (-1, 1, 0):
-        for dy, dx in AROUND:
-            if (dz, dy, dx) != (0, 0, 0):
-                ok = inside(dy, dx) & (g + dz >= 0) & (g + dz < n_gz)
-                greeted += greet(ok, (g + dz, y + dy, x + dx))
-
-    def band(ref, r):
-        return ref.at[pl.ds(pl.multiple_of(r * PATCH, PATCH), PATCH), :]
+    for ok, device in near:
+        greeted += told(barrier, ok, device)
+
+    def band(ref, k):
+        rows = pl.ds(pl.multiple_of(k // (PER // Q) * PATCH, PATCH), PATCH)
+        return ref.at[rows, pl.ds(pl.multiple_of(k % (PER // Q) * WIDTH, WIDTH), WIDTH)]
 
     table_copies = [
         pltpu.make_async_copy(src, dst, table_sem.at[i])
@@ -252,7 +257,7 @@
     ]
     for copy in table_copies[:2]:
         copy.start()
-    for r in range(PER):
+    for r in range(PIECES):
         pltpu.make_async_copy(band(images.at[0], r), own.at[r], own_sem.at[r]).start()
     for copy in table_copies[2:]:
         copy.start()
@@ -260,7 +265,7 @@
         anchor.at[0], ties.at[1, pl.ds(SWEEPS, NODES), :], tie_sem.at[slot(0, 0)]
     )
     tie_own.start()
-    for r in range(PER):
+    for r in range(PIECES):
 
         @pl.when(g == 0)
         def _():
@@ -269,37 +274,6 @@
         @pl.when(g == n_gz - 1)
         def _():
             pltpu.make_async_copy(band(boundary, r), after.at[r], after_sem.at[r]).start()
-
-    ramp_rows = iota((8, NODES), 1).astype(f32)
-    for t in range(n_gz):
-
-        @pl.when(t >= g)
-        def _():
-            land_in[t] = ramp_rows
-
-    for edge, count, first in ((y == 0, SWEEPS, 0), (y == n_ty - 1, SWEEPS, SWEEPS + NODES)):
-
-        @pl.when(edge)
-        def _():
-            for d in range(3):
-                ties[d, pl.ds(first, count), :] = jnp.zeros((count, NODES), f32)
-
-    for edge, d in ((x == 0, 0), (x == n_tx - 1, 2)):
-
-        @pl.when(edge)
-        def _():
-            ties[d] = jnp.zeros((WIDE, NODES), f32)
-
-    for dy, dx in AROUND:
-        if (dy, dx) != (0, 0):
-
-            @pl.when(jnp.logical_not(inside(dy, dx)))
-            def _():
-                patch_in[slot(dy, dx)] = jnp.zeros((8, NODES), f32)
-
-        @pl.when(jnp.logical_not(inside(dy, dx)) | (g < 2))
-        def _():
-            patch_in[9 + slot(dy, dx)] = jnp.zeros((8, NODES), f32)
 
     pl.semaphore_wait(barrier, greeted)
 
@@ -314,7 +288,7 @@
     def to_earlier(r):
         return remote(band(images.at[0], r), after.at[r], down_sem.at[r], after_sem.at[r], (g - 1, y, x))
 
-    for r in range(PER):
+    for r in range(PIECES):
 
         @pl.when(g < n_gz - 1)
         def _():
@@ -338,12 +312,48 @@
             (g, y + dy, x + dx),
         )
 
-    for dy, dx in AROUND:
-        if (dy, dx) != (0, 0):
+    def send_ties(steps):
+        for dy, dx in steps:
 
             @pl.when(inside(dy, dx))
             def _():
                 tie_copy(dy, dx).start()
+
+    send_ties(SIDES)
+    passed = jnp.int32(0)
+    for ok, device in near:
+        passed += told(rounds.at[0], ok, device)
+
+    ramp_rows = iota((8, NODES), 1).astype(f32)
+    for t in range(n_gz):
+
+        @pl.when(t >= g)
+        def _():
+            land_in[t] = ramp_rows
+
+    for edge, count, first in ((y == 0, SWEEPS, 0), (y == n_ty - 1, SWEEPS, SWEEPS + NODES)):
+
+        @pl.when(edge)
+        def _():
+            for d in range(3):
+                ties[d, pl.ds(first, count), :] = jnp.zeros((count, NODES), f32)
+
+    for edge, d in ((x == 0, 0), (x == n_tx - 1, 2)):
+
+        @pl.when(edge)
+        def _():
+            ties[d] = jnp.zeros((WIDE, NODES), f32)
+
+    for dy, dx in AROUND:
+        if (dy, dx) != (0, 0):
+
+            @pl.when(jnp.logical_not(inside(dy, dx)))
+            def _():
+                patch_in[slot(dy, dx)] = jnp.zeros((8, NODES), f32)
+
+        @pl.when(jnp.logical_not(inside(dy, dx)) | (g < 2))
+        def _():
+            patch_in[9 + slot(dy, dx)] = jnp.zeros((8, NODES), f32)
 
     def arrival(ref, sem):
         pltpu.make_async_copy(ref, ref, sem).wait()
@@ -356,10 +366,86 @@
         spectra[r] = packed_spectrum(own[r], left, right)
         return carry
 
-    lax.fori_loop(0, PER, own_step, 0)
+    lax.fori_loop(0, PIECES // 2, own_step, 0)
+    pl.semaphore_wait(rounds.at[0], passed)
+    send_ties(CORNERS)
+    passed_on = jnp.int32(0)
+    for step in (-2, -1, 1, 2):
+        passed_on += told(rounds.at[1], within(step), (g + step, y, x))
+    lax.fori_loop(PIECES // 2, PIECES, own_step, 0)
+    pl.semaphore_wait(rounds.at[1], passed_on)
+    told(rounds.at[2], within(-4), (g - 4, y, x))
 
     for copy in table_copies[2:]:
         copy.wait()
+
+    lag_rows = signed_lag((PATCH, PATCH), 0)
+
+    def softmax_sums(wide, k):
+        for at_pair in range(2 * Q):
+            pair, q = at_pair // Q, at_pair % Q
+            score = wide[:, at_pair * PATCH : (at_pair + 1) * PATCH]
+            weight = jnp.exp2(score - jnp.max(score))
+            at = pl.ds((k % (PER // Q) * Q + q) * PER + k // (PER // Q), 1)
+            sums[pair, 0, at, :] = jnp.sum(weight, axis=0, keepdims=True)
+            sums[pair, 1, at, :] = jnp.sum(weight * lag_rows, axis=0, keepdims=True)
+
+    def band_step(k, carry):
+        arrival(before.at[k], before_sem.at[k])
+        arrival(after.at[k], after_sem.at[k])
+        pair = paired_spectrum(before[k], left, right_pair)
+        there = packed_spectrum(after[k], left, right)
+        products = [cross_spectrum(pair, spectra[k]), cross_spectrum(pair, there)]
+        softmax_sums(scores(jnp.concatenate(products, axis=0), back_right, back_left), k)
+        return carry
+
+    lax.fori_loop(0, PIECES, band_step, 0)
+
+    lag_lanes = signed_lag((PER * PER, PATCH), 1)
+    col_of = iota((PER * PER, 128), 1) - iota((PER * PER, 128), 0) // PER
+
+    def flow(pair):
+        weight = sums[pair, 0]
+        scale = (1.0 / STRIDE) / jnp.sum(weight, axis=1, keepdims=True)
+        rows = jnp.sum(sums[pair, 1], axis=1, keepdims=True) * scale
+        cols = jnp.sum(weight * lag_lanes, axis=1, keepdims=True) * scale
+        return rows, cols
+
+    def patch_tile(rows, cols):
+        part = jnp.where(col_of == 0, rows, jnp.where(col_of == PER, cols, 0.0))
+        part = part[:8] + part[8:]
+        return part + pltpu.roll(part, 4, 0)
+
+    nearer, farther = flow(0), flow(1)
+    near_scale = jnp.where(g >= 2, 0.5, 1.0).astype(f32)
+    for kind, flows in ((1, [0.5 * (b - a) for a, b in zip(nearer, farther)]), (0, [near_scale * v for v in nearer])):
+        tile = patch_tile(*flows)
+        for d in range(3):
+            value = tile if d == 0 else pltpu.roll(tile, 8 * d, 1)
+            patch_out[kind, d] = value
+            if (kind, d) == (0, 1):
+                patch_in[slot(0, 0)] = value
+
+    def patch_copy(kind, dy, dx):
+        to = 9 * kind + slot(-dy, -dx)
+        return remote(
+            patch_out.at[kind, 1 - dx], patch_in.at[to], patch_sent.at[to], patch_sem.at[to],
+            (g + kind, y + dy, x + dx),
+        )
+
+    ahead = (g >= 1) & (g < n_gz - 1)
+    for dy, dx in sorted(AROUND, key=lambda d: -abs(d[0]) - abs(d[1])):
+
+        @pl.when(inside(dy, dx) & ahead)
+        def _():
+            patch_copy(1, dy, dx).start()
+
+        if (dy, dx) != (0, 0):
+
+            @pl.when(inside(dy, dx))
+            def _():
+                patch_copy(0, dy, dx).start()
+
     tie_own.wait()
     for dy, dx in AROUND:
         if (dy, dx) != (0, 0):
@@ -392,73 +478,9 @@
             rate[group, :, u * 128 : (u + 1) * 128] = held
             pull[group, :, u * 128 : (u + 1) * 128] = value * held
 
-    lag_rows = signed_lag((PATCH, PATCH), 0)
-
-    def softmax_sums(wide, pair, r):
-        for q in range(PER):
-            score = wide[:, q * PATCH : (q + 1) * PATCH]
-            weight = jnp.exp2(score - jnp.max(score))
-            at = pl.ds(q * PER + r, 1)
-            sums[pair, 0, at, :] = jnp.sum(weight, axis=0, keepdims=True)
-            sums[pair, 1, at, :] = jnp.sum(weight * lag_rows, axis=0, keepdims=True)
-
-    def band_step(r, carry):
-        arrival(before.at[r], before_sem.at[r])
-        arrival(after.at[r], after_sem.at[r])
-        pair = paired_spectrum(before[r], left, right_pair)
-        there = packed_spectrum(after[r], left, right)
-        near = scores(cross_spectrum(pair, spectra[r]), back_right, back_left)
-        far = scores(cross_spectrum(pair, there), back_right, back_left)
-        softmax_sums(near, 0, r)
-        softmax_sums(far, 1, r)
-        return carry
-
-    lax.fori_loop(0, PER, band_step, 0)
-
-    lag_lanes = signed_lag((PER * PER, PATCH), 1)
-    col_of = iota((PER * PER, 128), 1) - iota((PER * PER, 128), 0) // PER
-
-    def flow(pair):
-        weight = sums[pair, 0]
-        scale = (1.0 / STRIDE) / jnp.sum(weight, axis=1, keepdims=True)
-        rows = jnp.sum(sums[pair, 1], axis=1, keepdims=True) * scale
-        cols = jnp.sum(weight * lag_lanes, axis=1, keepdims=True) * scale
-        return rows, cols
-
-    def patch_tile(rows, cols):
-        part = jnp.where(col_of == 0, rows, jnp.where(col_of == PER, cols, 0.0))
-        part = part[:8] + part[8:]
-        return part + pltpu.roll(part, 4, 0)
-
-    near, far = flow(0), flow(1)
-    near_scale = jnp.where(g >= 2, 0.5, 1.0).astype(f32)
-    for kind, flows in ((1, [0.5 * (b - a) for a, b in zip(near, far)]), (0, [near_scale * v for v in near])):
-        tile = patch_tile(*flows)
-        for d in range(3):
-            value = tile if d == 0 else pltpu.roll(tile, 8 * d, 1)
-            patch_out[kind, d] = value
-            if (kind, d) == (0, 1):
-                patch_in[slot(0, 0)] = value
-
-    def patch_copy(kind, dy, dx):
-        to = 9 * kind + slot(-dy, -dx)
-        return remote(
-            patch_out.at[kind, 1 - dx], patch_in.at[to], patch_sent.at[to], patch_sem.at[to],
-            (g + kind, y + dy, x + dx),
-        )
-
-    ahead = (g >= 1) & (g < n_gz - 1)
-    for dy, dx in sorted(AROUND, key=lambda d: -abs(d[0]) - abs(d[1])):
-
-        @pl.when(inside(dy, dx) & ahead)
-        def _():
-            patch_copy(1, dy, dx).start()
-
-        if (dy, dx) != (0, 0):
-
-            @pl.when(inside(dy, dx))
-            def _():
-                patch_copy(0, dy, dx).start()
+    @pl.when(within(4))
+    def _():
+        pl.semaphore_wait(rounds.at[2], 1)
 
     for dy, dx in AROUND:
 
@@ -538,7 +560,7 @@
     mesh_out[1] = cols
     land_all[n_gz] = landing
 
-    for r in range(PER):
+    for r in range(PIECES):
 
         @pl.when(g < n_gz - 1)
         def _():
@@ -616,10 +638,10 @@
             in_specs=[hbm] * (3 + len(constants)),
             out_specs=(vmem, vmem),
             scratch_shapes=[
-                pltpu.VMEM((PER, PATCH, TILE), bf16),
-                pltpu.VMEM((PER, PATCH, TILE), bf16),
-                pltpu.VMEM((PER, PATCH, TILE), bf16),
-                pltpu.VMEM((PER, PER * PATCH, PATCH), f32),
+                pltpu.VMEM((PIECES, PATCH, WIDTH), bf16),
+                pltpu.VMEM((PIECES, PATCH, WIDTH), bf16),
+                pltpu.VMEM((PIECES, PATCH, WIDTH), bf16),
+                pltpu.VMEM((PIECES, WIDTH, PATCH), f32),
                 pltpu.VMEM((3, WIDE, NODES), f32),
                 pltpu.VMEM((18, 8, NODES), f32),
                 pltpu.VMEM((2, 3, 8, NODES), f32),
@@ -632,17 +654,18 @@
                 pltpu.VMEM((GROUPS, 8, LANES), f32),
                 *(pltpu.VMEM(c.shape, bf16) for c in constants),
                 dma((len(constants),)),
-                dma((PER,)),
-                dma((PER,)),
-                dma((PER,)),
-                dma((PER,)),
-                dma((PER,)),
+                dma((PIECES,)),
+                dma((PIECES,)),
+                dma((PIECES,)),
+                dma((PIECES,)),
+                dma((PIECES,)),
                 dma((9,)),
                 dma((9,)),
                 dma((18,)),
                 dma((18,)),
                 dma((n_gz,)),
                 dma((n_gz,)),
+                pltpu.SemaphoreType.REGULAR((3,)),
             ],
             compiler_params=pltpu.CompilerParams(
                 collective_id=0, has_side_effects=True, vmem_limit_bytes=GRANT

time: 29.4 us -> 27.1 us (0.922)
  Pallas kernels: 28.6 us -> 26.4 us
    pallas_call x1, Pallas kernels: 27.4 us -> 25.2 us  [local(): pl.pallas_call(functools.partial(kernel, sizes), out_shape=(jax.ShapeDtyp...]
where the time goes in v2:
time: 27.1 us; the launch traced here: 27 us
  Pallas kernels  26.4 us (97%)
  between operations  0.64 us (2%)
    pallas_call x1, Pallas kernels, local(): pl.pallas_call(functools.partial(kernel, sizes), out_shape=(jax.ShapeDtyp...  25.2 us
    pallas_call x1, Pallas kernels, local(): pl.pallas_call(functools.partial(finish, n_gz), out_shape=(jax.ShapeDtype...  1.23 us

profile of v2, /device:TPU:70, one launch (start us, length us, event | category | flops | bytes accessed | tf_op | source)
XLA Modules:
  0.0 27.0 jit_solution(12837935726803230400)
XLA Ops:
  0.6 25.2 %align.1 = (f32[2,128,128]{2,1,0:T(8,128)S(1)}, f32[9,8,128]{2,1,0:T(8,128)S(1)}) custom-call(bf16[1,512,512]{2,1,0:T(8,128)(2,1)} %images.1, bf16[512,512]{1,0:T(8,128)(2,1)} %boundary.1, f32[1,128,128]{2,1,0:T(8,128)} %anchor.1, bf16[256,128]{1,0:T(8,128)(2,1)} %constant.18.clone.rest_0_, bf16[256,256]{1,0:T(8,128)(2,1)} %constant.19.clone.rest_1_, ...), custom_call_target="tpu_custom_call" | custom-call | tf_op jit(solution)/shard_map/align/pallas_call | solution.py:632
  25.8 1.2 %finish.1 = (f32[1,2,128,128]{3,2,1,0:T(8,128)}, f32[1,1,1,2,128]{4,3,2,1,0:T(2,128)}) custom-call(f32[2,128,128]{2,1,0:T(8,128)S(1)} %get-tuple-element.4.mesh_in, f32[9,8,128]{2,1,0:T(8,128)S(1)} %get-tuple-element.5.land_all), custom_call_target="tpu_custom_call" | custom-call | tf_op jit(solution)/shard_map/finish/pallas_call | solution.py:675
